TPU v7x, 128 devices: a whole 4x4x4 slice. The times are simulated.
128 devices in a mesh: row: 8 (over z_hi, y), col: 16 (over z_lo, x, core).
Axes of the slice: x: 4, y: 4, z: 4 (z_hi: 2, z_lo: 2; z = z_hi * 2 + z_lo), core: 2. Of those that a mesh axis runs over, the one named last changes fastest.
Arguments:
- features: bfloat16 [65536, 256], P(('col', 'row')), may hold values from -6 to 6
- weight: bfloat16 [256, 256], replicated, may hold values from -0.375 to 0.375
- bias: float32 [256], replicated, may hold values from -4 to 4
- cotangent: bfloat16 [65536, 256], P(('row', 'col')), may hold values from -6 to 6
- tiles: bfloat16 [8, 16, 384, 128, 128], P('row', 'col'), may hold values from -0.0546875 to 0.0546875
- tile_rows: int32 [8, 16, 384], P('row', 'col'), may hold values from 0 to 63, as said below
- tile_cols: int32 [8, 16, 384], P('row', 'col'), may hold values from 0 to 31
- tile_counts: int32 [8, 16], P('row', 'col'), may hold values from 24 to 384, as said below
Outputs:
- hidden: bfloat16 [65536, 256], P(('row', 'col'))
- grad_weight: float32 [256, 256], replicated
- grad_bias: float32 [256], replicated
- grad_features: bfloat16 [65536, 256], P(('col', 'row'))
Inputs may be any that keep to these rules, and one draw needn't show every extreme that they name: `tile_rows`: on each grid cell the slots name distinct blocks. `tile_counts`: slots at or after a cell's count are unused; some cell uses all 384 slots.
All inputs are finite; a program needn't handle non-finite values.
Results may differ from a plain program's by a relative error of at most 0.013.
Values may be sent and summed in bfloat16 or wider, within the bound.
A program may use at most 128 MiB of HBM per device.

v0:
```python
import math
import jax
import jax.numpy as jnp
from jax import lax
from jax.sharding import PartitionSpec as P


def accumulate(tiles, dest_ids, source_ids, live_count, source_blocks, out_blocks, backward):
    slots = tiles.shape[0]
    group = math.gcd(slots, 32)
    block = tiles.shape[-1]
    width = source_blocks.shape[-1]
    in_blocks = source_blocks.shape[0]
    flat_source = source_blocks.reshape(in_blocks, block * width)
    in_range = jnp.arange(in_blocks, dtype=jnp.int32)
    out_range = jnp.arange(out_blocks, dtype=jnp.int32)

    def one_group(step_index, total):
        start = step_index * group
        tile_group = lax.dynamic_slice_in_dim(tiles, start, group, 0)
        dest_group = lax.dynamic_slice_in_dim(dest_ids, start, group, 0)
        source_group = lax.dynamic_slice_in_dim(source_ids, start, group, 0)
        live = start + jnp.arange(group, dtype=jnp.int32) < live_count
        if backward:
            fetch_ids = dest_group
            target = source_group
        else:
            fetch_ids = source_group
            target = dest_group
        picker = (fetch_ids[:, None] == in_range[None, :]).astype(jnp.bfloat16)
        fetched = jnp.dot(picker, flat_source, preferred_element_type=jnp.float32)
        fetched = fetched.astype(jnp.bfloat16).reshape(group, block, width)
        if backward:
            contrib = jnp.einsum(
                "tji,tjf->tif", tile_group, fetched, preferred_element_type=jnp.float32
            )
        else:
            contrib = jnp.einsum(
                "tij,tjf->tif", tile_group, fetched, preferred_element_type=jnp.float32
            )
        placer = ((target[:, None] == out_range[None, :]) & live[:, None]).astype(jnp.float32)
        added = jnp.dot(
            placer.T,
            contrib.reshape(group, block * width),
            precision=lax.Precision.HIGHEST,
            preferred_element_type=jnp.float32,
        )
        return total + added

    start_total = jnp.zeros((out_blocks, block * width), jnp.float32)
    result = lax.fori_loop(0, slots // group, one_group, start_total)
    return result.reshape(out_blocks, block, width)


def per_device(features, weight, bias, cotangent, tiles, tile_rows, tile_cols, tile_counts):
    tile_set = tiles[0, 0]
    dest_ids = tile_rows[0, 0]
    source_ids = tile_cols[0, 0]
    live_count = tile_counts[0, 0]
    block = tile_set.shape[-1]
    own_nodes = features.shape[0]
    width = features.shape[1]
    row_count = lax.axis_size("row")
    col_count = lax.axis_size("col")
    blocks_down = own_nodes * col_count // block
    blocks_across = own_nodes * row_count // block
    factor = 1.0 / math.sqrt(own_nodes * row_count * col_count)
    panel = lax.all_gather(features, "row", axis=0, tiled=True)
    panel_blocks = panel.reshape(blocks_across, block, width)
    partial_value = accumulate(
        tile_set, dest_ids, source_ids, live_count, panel_blocks, blocks_down, False
    )
    term = partial_value.reshape(blocks_down * block, width)
    summed = lax.psum_scatter(term, "col", scatter_dimension=0, tiled=True)
    aggregated = summed.astype(jnp.bfloat16)
    preact = jnp.dot(aggregated, weight, preferred_element_type=jnp.float32) + bias
    hidden = jax.nn.silu(preact).astype(jnp.bfloat16)
    sigma = jax.nn.sigmoid(preact)
    slope = sigma * (1.0 + preact * (1.0 - sigma))
    grad_pre = (cotangent.astype(jnp.float32) * slope).astype(jnp.bfloat16)
    local_weight = jnp.einsum("nf,ng->fg", aggregated, grad_pre, preferred_element_type=jnp.float32)
    local_bias = jnp.sum(grad_pre.astype(jnp.float32), axis=0)
    grad_agg = jnp.dot(grad_pre, weight.T, preferred_element_type=jnp.float32).astype(jnp.bfloat16)
    grad_panel = lax.all_gather(grad_agg, "col", axis=0, tiled=True)
    grad_blocks = grad_panel.reshape(blocks_down, block, width)
    partial_back = accumulate(
        tile_set, dest_ids, source_ids, live_count, grad_blocks, blocks_across, True
    )
    term_back = partial_back.reshape(blocks_across * block, width)
    grad_features = lax.psum_scatter(
        term_back.astype(jnp.bfloat16), "row", scatter_dimension=0, tiled=True
    )
    grad_weight, grad_bias = lax.psum((local_weight, local_bias), ("row", "col"))
    grad_weight = grad_weight * factor
    grad_bias = grad_bias * factor
    return (hidden, grad_weight, grad_bias, grad_features)


def solution(mesh):
    in_specs = (
        P(("col", "row"), None),
        P(),
        P(),
        P(("row", "col"), None),
        P("row", "col", None, None, None),
        P("row", "col", None),
        P("row", "col", None),
        P("row", "col"),
    )
    out_specs = (P(("row", "col"), None), P(), P(), P(("col", "row"), None))
    return jax.shard_map(
        per_device, mesh=mesh, in_specs=in_specs, out_specs=out_specs, check_vma=False
    )
```

profile of v0, /device:TPU:0, one launch (start us, length us, event | category | flops | bytes accessed | tf_op | source)
XLA Modules:
  0.0 667.1 jit_solution(5247763881698745133)
XLA Ops:
  9.4 58.5 %all-gather.3.cloned.1.call-done = bf16[4096,256]{1,0:T(8,128)(2,1)} async-done(((bf16[512,256]{1,0:T(8,128)(2,1)}), bf16[4096,256]{1,0:T(8,128)(2,1)}) %all-gather.3.cloned.1.call-update) | async-done | bytes 2097168 | tf_op jit(solution)/shard_map/all_gather | solution.py:68
  70.7 196.6 %while.28 = (s32[]{:T(128)}, f32[64,32768]{1,0:T(8,128)}, s32[384]{0:T(512)S(1)}, s32[]{:T(128)}, bf16[384,128,128]{2,1,0:T(8,128)(2,1)}, /*index=5*/s32[384]{0:...) while((s32[]{:T(128)}, f32[64,32768]{1,0:T(8,128)}, ...), condition=%wide.region_1.0_spmd.clone, body=%wide.region_0.0_spmd.clone.sunk | while | flops 1146098688 | bytes 103810120 | solution.py:51
  77.4 6.5 convolution_add_fusion.5
  93.8 6.5 convolution_add_fusion.5
  110.1 6.5 convolution_add_fusion.5
  126.5 6.5 convolution_add_fusion.5
  142.9 6.5 convolution_add_fusion.5
  159.3 6.5 convolution_add_fusion.5
  175.7 6.5 convolution_add_fusion.5
  192.0 6.5 convolution_add_fusion.5
  208.4 6.5 convolution_add_fusion.5
  224.8 6.5 convolution_add_fusion.5
  241.2 6.5 convolution_add_fusion.5
  257.6 6.5 convolution_add_fusion.5
  267.3 9.2 %reshape_reshape.11 = f32[8192,256]{1,0:T(8,128)} reshape(f32[64,32768]{1,0:T(8,128)} %get-tuple-element.312) | data formatting | bytes 16777216 | tf_op jit(solution)/shard_map/reshape;reshape | solution.py:73
  276.6 73.4 %reduce-scatter.3.cloned.1.call-done = f32[512,256]{1,0:T(8,128)} async-done(((f32[8192,256]{1,0:T(8,128)}), f32[512,256]{1,0:T(8,128)}) %reduce-scatter.3.cloned.1.call-update) | async-done | bytes 524304 | tf_op jit(solution)/shard_map/reduce_scatter | solution.py:74
  353.4 16.7 %copy.12 = bf16[1,1,384,128,128]{3,4,2,1,0:T(8,128)(2,1)} copy(bf16[1,1,384,128,128]{4,3,2,1,0:T(8,128)(2,1)} %bitcast.60) | data formatting | bytes 25165824 | tf_op args[4]
  371.2 18.1 %all-gather.5.cloned.1.call-done = bf16[8192,256]{1,0:T(8,128)(2,1)} async-done(((bf16[512,256]{1,0:T(8,128)(2,1)}), bf16[8192,256]{1,0:T(8,128)(2,1)}) %all-gather.5.cloned.1.call-update) | async-done | bytes 4194320 | tf_op jit(solution)/shard_map/all_gather | solution.py:84
  389.2 7.4 %reshape_reshape.12 = bf16[64,32768]{1,0:T(8,128)(2,1)} reshape(bf16[8192,256]{1,0:T(8,128)(2,1)} %all-gather.5.cloned.1.call-done) | data formatting | bytes 8388608 | tf_op jit(solution)/shard_map/reshape;reshape | solution.py:14
  396.6 183.3 %while.29 = (s32[]{:T(128)}, f32[32,32768]{1,0:T(8,128)}, s32[384]{0:T(512)S(1)}, s32[]{:T(128)}, bf16[384,128,128]{1,2,0:T(8,128)(2,1)}, /*index=5*/s32[384]{0:...) while((s32[]{:T(128)}, f32[32,32768]{1,0:T(8,128)}, ...), condition=%wide.region_7.8_spmd.clone, body=%wide.region_6.7_spmd.clone.sunk | while | flops 808456256 | bytes 72352824 | solution.py:51
  405.3 4.7 convolution_add_fusion.6
  420.6 4.7 convolution_add_fusion.6
  435.8 4.7 convolution_add_fusion.6
  451.1 4.7 convolution_add_fusion.6
  466.4 4.7 convolution_add_fusion.6
  481.7 4.7 convolution_add_fusion.6
  496.9 4.7 convolution_add_fusion.6
  512.2 4.7 convolution_add_fusion.6
  542.7 4.7 convolution_add_fusion.6
  558.0 4.7 convolution_add_fusion.6
  573.3 4.7 convolution_add_fusion.6
  584.7 69.3 %psum.15 = f32[256]{0:T(256)S(1)} all-reduce(f32[256]{0:T(256)S(1)} %get-tuple-element.405), channel_id=1, replica_groups=mesh['row'=8,'col'=16] {'row','col'}, use_global_device_ids=true, to_apply=%region_5.6 | all-reduce | flops 256 | bytes 2048 | tf_op jit(solution)/shard_map/psum | solution.py:93
  (335 shorter events, 269.5 us)
Async XLA Ops:
  7.2 342.9 %copy-start = (bf16[256,256]{1,0:T(8,128)(2,1)S(1)}, bf16[256,256]{1,0:T(8,128)(2,1)}, u32[]{:S(2)}) copy-start(bf16[256,256]{1,0:T(8,128)(2,1)} %param.13) | copy-start | bytes 393220
  7.2 60.7 %all-gather.3.cloned.1.call-start = ((), (), s32[]{:S(2)}) async-start(), calls=%async_computation.2 | async-start | bytes 2359296 | tf_op jit(solution)/shard_map/all_gather | solution.py:68
  7.9 342.1 %reduce-scatter.3.cloned.1.call-start = ((), (), s32[]{:S(2)}) async-start(), calls=%async_computation.3 | async-start | bytes 8912896 | tf_op jit(solution)/shard_map/reduce_scatter | solution.py:74
  72.8 4.5 slice-start
  83.9 3.2 copy-start.2
  89.2 4.5 slice-start
  100.3 3.2 copy-start.2
  105.6 4.5 slice-start
  116.7 3.2 copy-start.2
  122.0 4.5 slice-start
  133.0 3.2 copy-start.2
  138.3 4.5 slice-start
  154.7 4.5 slice-start
  165.8 3.2 copy-start.2
  171.1 4.5 slice-start
  182.2 3.2 copy-start.2
  187.5 4.5 slice-start
  203.8 4.5 slice-start
  214.9 3.2 copy-start.2
  220.2 4.5 slice-start
  231.3 3.2 copy-start.2
  236.6 4.5 slice-start
  247.7 3.2 copy-start.2
  253.0 4.5 slice-start
  264.1 3.2 copy-start.2
  276.6 73.5 %copy-start.6 = (bf16[512,256]{1,0:T(8,128)(2,1)S(1)}, bf16[512,256]{1,0:T(8,128)(2,1)}, u32[]{:S(2)}) copy-start(bf16[512,256]{1,0:T(8,128)(2,1)} %param.15) | copy-start | bytes 786436
  276.6 73.5 %copy-start.7 = (f32[256]{0:T(256)S(1)}, f32[256]{0:T(256)}, u32[]{:S(2)}) copy-start(f32[256]{0:T(256)} %param.14) | copy-start | bytes 3076
  276.6 112.7 %all-gather.5.cloned.1.call-start = ((), (), s32[]{:S(2)}) async-start(), calls=%async_computation.5 | async-start | bytes 4456448 | tf_op jit(solution)/shard_map/all_gather | solution.py:84
  353.2 301.4 %all-reduce.2.cloned.1.call-start = ((), (), s32[]{:S(2)}) async-start(), calls=%async_computation.4 | async-start | bytes 524288 | tf_op jit(solution)/shard_map/psum | solution.py:93
  353.4 16.7 %copy-start.5 = (f32[512,256]{1,0:T(8,128)S(1)}, f32[512,256]{1,0:T(8,128)}, u32[]{:S(2)}) copy-start(f32[512,256]{1,0:T(8,128)} %reduce-scatter.3.cloned.1.call-done) | copy-start | bytes 1572868
  371.1 289.5 %reduce-scatter.5.cloned.1.call-start = ((), (), s32[]{:S(2)}) async-start(), calls=%async_computation.6 | async-start | bytes 2359296 | tf_op jit(solution)/shard_map/reduce_scatter | solution.py:90
  579.9 80.7 %copy-start.1 = (bf16[256,256]{1,0:T(8,128)(2,1)S(1)}, bf16[256,256]{1,0:T(8,128)(2,1)}, u32[]{:S(2)}) copy-start(bf16[256,256]{1,0:T(8,128)(2,1)} %param.13) | copy-start | bytes 393220
  (38 other events, 88.7 us)
Sparse Core Ops, SparseCore 0:
  10.4 57.4 all-gather.2
  276.7 73.2 reduce-scatter.2
  353.3 35.9 all-gather.4
  394.4 141.9 all-reduce.1
  584.8 75.7 reduce-scatter.4
where the time goes:
time: 669 us; the launch traced here: 667 us
  matrix products  231 us (35%)
  local copies, waits for them, and re-layouts  174 us (26%)
  waiting for transfers between devices  155 us (23%)
  blocking collectives  69.3 us (10%)
  other arithmetic  21.7 us (3%)
  between operations  13.8 us (2%)
    dot_general x24, matrix products, one_group(): jnp.dot(placer.T, contrib.reshape(group, block * width), precision=lax.Pr...  134 us
    while x168, local copies, waits for them, and re-layouts  132 us
    reduce_scatter x1, waiting for transfers between devices, per_device(): summed = lax.psum_scatter(term, 'col', scatter_dimension=0, tiled=True)  73.4 us
    psum x1, blocking collectives, per_device(): lax.psum((local_weight, local_bias), ('row', 'col'))  69.3 us
    all_gather x1, waiting for transfers between devices, per_device(): panel = lax.all_gather(features, 'row', axis=0, tiled=True)  58.5 us
    dot_general x24, matrix products, one_group(): fetched = jnp.dot(picker, flat_source, preferred_element_type=jnp.float32)  44.3 us
    dot_general x12, matrix products, one_group(): jnp.einsum('tij,tjf->tif', tile_group, fetched, preferred_element_type=jn...  25 us
    dot_general x12, matrix products, one_group(): jnp.einsum('tji,tjf->tif', tile_group, fetched, preferred_element_type=jn...  23.2 us
  transfers between devices with their start and end apart: 5, of which 4 were waited for; matrix products, arithmetic and copies ran while one was open for 29% of the time, Pallas kernels for 0%

commit v1 on v0

--- a/solution.py
+++ b/solution.py
@@ -90,7 +90,7 @@
     grad_features = lax.psum_scatter(
         term_back.astype(jnp.bfloat16), "row", scatter_dimension=0, tiled=True
     )
-    grad_weight, grad_bias = lax.psum((local_weight, local_bias), ("row", "col"))
+    grad_weight, grad_bias = lax.psum(lax.psum((local_weight, local_bias), "col"), "row")
     grad_weight = grad_weight * factor
     grad_bias = grad_bias * factor
     return (hidden, grad_weight, grad_bias, grad_features)

time: 669 us -> 790 us (1.18)
  waiting for transfers between devices: 155 us -> 291 us
  blocking collectives: 69.3 us -> 53.6 us
    psum x1 -> x2, waiting for transfers between devices: 0.01 us -> 97.3 us  [the longest x1 97.3 us: per_device(): lax.psum((local_weight, local_bias), 'col')]
    all_gather x1, waiting for transfers between devices: 18.1 us -> 40.8 us  [per_device(): grad_panel = lax.all_gather(grad_agg, 'col', axis=0, tiled=True)]
    psum x1 -> x2, blocking collectives: 69.3 us -> 53.6 us  [the longest x1 29.3 us: per_device(): lax.psum((local_weight, local_bias), 'col')]
    reduce_scatter x1, waiting for transfers between devices: 4.32 us -> 19.9 us  [per_device(): lax.psum_scatter(term_back.astype(jnp.bfloat16), 'row', scatter_dimension...]
    unnamed x11 -> x9, local copies, waits for them, and re-layouts: 16.7 us -> 16.7 us
  transfers between devices with their start and end apart: 5 -> 6, of which waited for: 4 -> 5; matrix products, arithmetic and copies ran while one was open for 29% -> 24% of each run, Pallas kernels for 0% -> 0%
where the time goes in v1:
time: 790 us; the launch traced here: 788 us
  waiting for transfers between devices  291 us (37%)
  matrix products  232 us (29%)
  local copies, waits for them, and re-layouts  174 us (22%)
  blocking collectives  53.6 us (7%)
  other arithmetic  21.7 us (3%)
  between operations  14.2 us (2%)
    dot_general x24, matrix products, one_group(): jnp.dot(placer.T, contrib.reshape(group, block * width), precision=lax.Pr...  134 us
    while x168, local copies, waits for them, and re-layouts  132 us
    psum x1, waiting for transfers between devices, per_device(): lax.psum((local_weight, local_bias), 'col')  97.3 us
    reduce_scatter x1, waiting for transfers between devices, per_device(): summed = lax.psum_scatter(term, 'col', scatter_dimension=0, tiled=True)  73.4 us
    all_gather x1, waiting for transfers between devices, per_device(): panel = lax.all_gather(features, 'row', axis=0, tiled=True)  58.5 us
    dot_general x24, matrix products, one_group(): fetched = jnp.dot(picker, flat_source, preferred_element_type=jnp.float32)  44.3 us
    all_gather x1, waiting for transfers between devices, per_device(): grad_panel = lax.all_gather(grad_agg, 'col', axis=0, tiled=True)  40.8 us
    psum x1, blocking collectives, per_device(): lax.psum((local_weight, local_bias), 'col')  29.3 us
  transfers between devices with their start and end apart: 6, of which 5 were waited for; matrix products, arithmetic and copies ran while one was open for 24% of the time, Pallas kernels for 0%

profile of v1, /device:TPU:0, one launch (start us, length us, event | category | flops | bytes accessed | tf_op | source)
XLA Modules:
  0.0 788.1 jit_solution(10056470270507905791)
XLA Ops:
  9.4 58.5 %all-gather.3.cloned.1.call-done = bf16[4096,256]{1,0:T(8,128)(2,1)} async-done(((bf16[512,256]{1,0:T(8,128)(2,1)}), bf16[4096,256]{1,0:T(8,128)(2,1)}) %all-gather.3.cloned.1.call-update) | async-done | bytes 2097168 | tf_op jit(solution)/shard_map/all_gather | solution.py:68
  70.7 196.6 %while.28 = (s32[]{:T(128)}, f32[64,32768]{1,0:T(8,128)}, s32[384]{0:T(512)S(1)}, s32[]{:T(128)}, bf16[384,128,128]{2,1,0:T(8,128)(2,1)}, /*index=5*/s32[384]{0:...) while((s32[]{:T(128)}, f32[64,32768]{1,0:T(8,128)}, ...), condition=%wide.region_1.0_spmd.clone, body=%wide.region_0.0_spmd.clone.sunk | while | flops 1146098688 | bytes 103810120 | solution.py:51
  77.4 6.5 convolution_add_fusion.5
  93.8 6.5 convolution_add_fusion.5
  110.2 6.5 convolution_add_fusion.5
  126.5 6.5 convolution_add_fusion.5
  142.9 6.5 convolution_add_fusion.5
  159.3 6.5 convolution_add_fusion.5
  175.7 6.5 convolution_add_fusion.5
  192.1 6.5 convolution_add_fusion.5
  208.4 6.5 convolution_add_fusion.5
  224.8 6.5 convolution_add_fusion.5
  241.2 6.5 convolution_add_fusion.5
  257.6 6.5 convolution_add_fusion.5
  267.3 9.3 %reshape_reshape.11 = f32[8192,256]{1,0:T(8,128)} reshape(f32[64,32768]{1,0:T(8,128)} %get-tuple-element.312) | data formatting | bytes 16777216 | tf_op jit(solution)/shard_map/reshape;reshape | solution.py:73
  276.7 73.4 %reduce-scatter.3.cloned.1.call-done = f32[512,256]{1,0:T(8,128)} async-done(((f32[8192,256]{1,0:T(8,128)}), f32[512,256]{1,0:T(8,128)}) %reduce-scatter.3.cloned.1.call-update) | async-done | bytes 524304 | tf_op jit(solution)/shard_map/reduce_scatter | solution.py:74
  355.5 16.6 %copy.12 = bf16[1,1,384,128,128]{3,4,2,1,0:T(8,128)(2,1)} copy(bf16[1,1,384,128,128]{4,3,2,1,0:T(8,128)(2,1)} %bitcast.60) | data formatting | bytes 25165824 | tf_op args[4]
  372.2 97.3 %all-reduce.3.cloned.1.call-done = f32[256,256]{1,0:T(8,128)} async-done(((f32[256,256]{1,0:T(8,128)}), f32[256,256]{1,0:T(8,128)}) %all-reduce.3.cloned.1.call-update) | async-done | bytes 262160 | tf_op jit(solution)/shard_map/psum | solution.py:93
  469.5 40.8 %all-gather.5.cloned.1.call-done = bf16[8192,256]{1,0:T(8,128)(2,1)} async-done(((bf16[512,256]{1,0:T(8,128)(2,1)}), bf16[8192,256]{1,0:T(8,128)(2,1)}) %all-gather.5.cloned.1.call-update) | async-done | bytes 4194320 | tf_op jit(solution)/shard_map/all_gather | solution.py:84
  510.3 7.4 reshape_reshape.12
  517.7 183.0 %while.29 = (s32[]{:T(128)}, f32[32,32768]{1,0:T(8,128)}, s32[384]{0:T(512)S(1)}, s32[]{:T(128)}, bf16[384,128,128]{1,2,0:T(8,128)(2,1)}, /*index=5*/s32[384]{0:...) while((s32[]{:T(128)}, f32[32,32768]{1,0:T(8,128)}, ...), condition=%wide.region_9.10_spmd.clone, body=%wide.region_8.9_spmd.clone.sunk | while | flops 808456256 | bytes 72352824 | solution.py:51
  556.8 4.7 convolution_add_fusion.6
  572.1 4.7 convolution_add_fusion.6
  587.4 4.7 convolution_add_fusion.6
  602.6 4.7 convolution_add_fusion.6
  617.9 4.7 convolution_add_fusion.6
  633.1 4.7 convolution_add_fusion.6
  648.4 4.7 convolution_add_fusion.6
  678.9 4.7 convolution_add_fusion.6
  705.5 29.3 %psum.30 = f32[256]{0:T(256)S(1)} all-reduce(f32[256]{0:T(256)S(1)} %get-tuple-element.405), channel_id=1, replica_groups=mesh['row'=8,'col'=16] {'col'}, use_global_device_ids=true, to_apply=%region_6.7 | all-reduce | flops 256 | bytes 2048 | tf_op jit(solution)/shard_map/psum | solution.py:93
  734.9 24.3 %psum.31 = f32[256]{0:T(256)S(1)} all-reduce(f32[256]{0:T(256)S(1)} %psum.30), channel_id=1, replica_groups=mesh['row'=8,'col'=16] {'row'}, use_global_device_ids=true, to_apply=%region_7.8 | all-reduce | flops 256 | bytes 2048 | tf_op jit(solution)/shard_map/psum | solution.py:93
  761.4 19.9 %reduce-scatter.5.cloned.1.call-done = bf16[512,256]{1,0:T(8,128)(2,1)} async-done(((bf16[4096,256]{1,0:T(8,128)(2,1)}), bf16[512,256]{1,0:T(8,128)(2,1)}) %reduce-scatter.5.cloned.1.call-update) | async-done | bytes 262160 | tf_op jit(solution)/shard_map/reduce_scatter | solution.py:90
  (337 shorter events, 280.0 us)
Async XLA Ops:
  7.2 342.9 %copy-start = (bf16[256,256]{1,0:T(8,128)(2,1)S(1)}, bf16[256,256]{1,0:T(8,128)(2,1)}, u32[]{:S(2)}) copy-start(bf16[256,256]{1,0:T(8,128)(2,1)} %param.13) | copy-start | bytes 393220
  7.2 60.7 %all-gather.3.cloned.1.call-start = ((), (), s32[]{:S(2)}) async-start(), calls=%async_computation.2 | async-start | bytes 2359296 | tf_op jit(solution)/shard_map/all_gather | solution.py:68
  7.9 342.1 %reduce-scatter.3.cloned.1.call-start = ((), (), s32[]{:S(2)}) async-start(), calls=%async_computation.3 | async-start | bytes 8912896 | tf_op jit(solution)/shard_map/reduce_scatter | solution.py:74
  72.8 4.5 slice-start
  83.9 3.2 copy-start.2
  89.2 4.5 slice-start
  100.3 3.2 copy-start.2
  105.6 4.5 slice-start
  116.7 3.2 copy-start.2
  122.0 4.5 slice-start
  133.1 3.2 copy-start.2
  138.3 4.5 slice-start
  149.4 3.2 copy-start.2
  154.7 4.5 slice-start
  165.8 3.2 copy-start.2
  171.1 4.5 slice-start
  182.2 3.2 copy-start.2
  187.5 4.5 slice-start
  198.6 3.2 copy-start.2
  203.9 4.5 slice-start
  220.2 4.5 slice-start
  231.3 3.2 copy-start.2
  236.6 4.5 slice-start
  247.7 3.2 copy-start.2
  253.0 4.5 slice-start
  276.6 73.5 %copy-start.5 = (bf16[512,256]{1,0:T(8,128)(2,1)S(1)}, bf16[512,256]{1,0:T(8,128)(2,1)}, u32[]{:S(2)}) copy-start(bf16[512,256]{1,0:T(8,128)(2,1)} %param.15) | copy-start | bytes 786436
  276.6 73.5 %copy-start.6 = (f32[256]{0:T(256)S(1)}, f32[256]{0:T(256)}, u32[]{:S(2)}) copy-start(f32[256]{0:T(256)} %param.14) | copy-start | bytes 3076
  276.6 192.8 %all-reduce.3.cloned.1.call-start = ((), (), s32[]{:S(2)}) async-start(), calls=%async_computation.4 | async-start | bytes 524288 | tf_op jit(solution)/shard_map/psum | solution.py:93
  354.2 156.0 %all-gather.5.cloned.1.call-start = ((), (), s32[]{:S(2)}) async-start(), calls=%async_computation.6 | async-start | bytes 4456448 | tf_op jit(solution)/shard_map/all_gather | solution.py:84
  355.3 404.4 %all-reduce.5.cloned.1.call-start = ((), (), s32[]{:S(2)}) async-start(), calls=%async_computation.5 | async-start | bytes 524288 | tf_op jit(solution)/shard_map/psum | solution.py:93
  469.4 311.8 %reduce-scatter.5.cloned.1.call-start = ((), (), s32[]{:S(2)}) async-start(), calls=%async_computation.7 | async-start | bytes 2359296 | tf_op jit(solution)/shard_map/reduce_scatter | solution.py:90
  700.7 80.5 %copy-start.1 = (bf16[256,256]{1,0:T(8,128)(2,1)S(1)}, bf16[256,256]{1,0:T(8,128)(2,1)}, u32[]{:S(2)}) copy-start(bf16[256,256]{1,0:T(8,128)(2,1)} %param.13) | copy-start | bytes 393220
  (38 other events, 88.6 us)
Sparse Core Ops, SparseCore 0:
  10.4 57.4 all-gather.2
  276.7 73.2 reduce-scatter.2
  354.4 115.0 all-reduce.2
  471.7 38.5 all-gather.4
  512.7 84.6 all-reduce.4
  705.6 75.5 reduce-scatter.4
